TPU v7x, 256 devices: a whole 4x4x8 slice. The times are simulated.
256 devices in a mesh: wide: 16 (over y_hi, x, core), narrow: 16 (over z, y_lo).
Axes of the slice: x: 4, y: 4 (y_hi: 2, y_lo: 2; y = y_hi * 2 + y_lo), z: 8, core: 2. Of those that a mesh axis runs over, the one named last changes fastest.
Arguments:
- documents: bfloat16 [16384, 768], P('wide'), may hold values from -8 to 8
- label_weight: bfloat16 [32768, 768], P(('wide', 'narrow')), may hold values from -1 to 1
- sample_ids: int32 [32768], P(('wide', 'narrow')), may hold values from 0 to 2812280, as said below
- positive_cols: int32 [16384, 4], P('wide'), may hold values from 0 to 32767
- up_weight: bfloat16 [768, 3072], P(None, 'narrow'), may hold values from -0.21875 to 0.21875
- down_weight: bfloat16 [3072, 768], P('narrow'), may hold values from -0.109375 to 0.109375
Outputs:
- label_grad: float32 [32768, 768], P(('wide', 'narrow'))
- up_grad: float32 [768, 3072], P('wide', 'narrow')
- down_grad: float32 [3072, 768], P('narrow', 'wide')
Inputs may be any that keep to these rules, and one draw needn't show every extreme that they name: `sample_ids`: frequency ranks (0 is the most frequent of 2812281 labels), not falling along the sampled columns; frequent ranks repeat.
All inputs are finite; a program needn't handle non-finite values.
Results may differ from a plain program's by a relative error of at most 0.01.
Values may be sent and summed in bfloat16 or wider, within the bound.
No kernel may reach another device: no remote copies, remote signals or barrier semaphores. Data moves between devices by JAX's collectives and lax.ppermute only.
A program may use at most 64 MiB of HBM per device.

v0:
```python
from functools import partial
import jax
import jax.numpy as jnp
from jax import lax
from jax.sharding import PartitionSpec as P

CATALOG = 2812281


def from_behind(block, axis, distance):
    devices = range(lax.axis_size(axis))
    route = [((i - distance) % len(devices), i) for i in devices]
    return lax.ppermute(block, axis, route)


def expected_log(rank_ids, sampled):
    rank_float = rank_ids.astype(jnp.float32)
    return (
        jnp.log(jnp.float32(sampled))
        + jnp.log(jnp.log1p(1.0 / (rank_float + 1.0)))
        - jnp.log(jnp.log(jnp.float32(CATALOG) + 1.0))
    )


def absorb(row_state, logits):
    run_max, run_sum = row_state
    new_max = jnp.maximum(run_max, jnp.max(logits, axis=1))
    run_sum = run_sum * jnp.exp(run_max - new_max) + jnp.sum(
        jnp.exp(logits - new_max[:, None]), axis=1
    )
    return (new_max, run_sum)


def local(documents, label_weight, sample_ids, positive_cols, up_weight, down_weight):
    wide_count = lax.axis_size("wide")
    narrow_count = lax.axis_size("narrow")
    wide_place = lax.axis_index("wide")
    narrow_place = lax.axis_index("narrow")
    lab_rows, model_width = label_weight.shape
    doc_rows = documents.shape[0]
    sampled = lab_rows * wide_count * narrow_count
    contract_rows = (((1,), (1,)), ((), ()))
    contract_first = (((0,), (0,)), ((), ()))
    pre_act = jnp.dot(documents, up_weight, preferred_element_type=jnp.float32)
    hidden = jax.nn.gelu(pre_act, approximate=False).astype(jnp.bfloat16)
    partial_out = jnp.dot(hidden, down_weight, preferred_element_type=jnp.float32)
    summed = lax.psum(partial_out, "narrow")
    embedding = (documents.astype(jnp.float32) + summed).astype(jnp.bfloat16)
    all_ranks = lax.all_gather(sample_ids, "wide", axis=0, tiled=True)
    log_expect = expected_log(all_ranks, sampled).reshape(wide_count, lab_rows)
    offsets = jnp.arange(lab_rows, dtype=jnp.int32)

    def block_logits(label_block, log_part):
        return (
            lax.dot_general(
                embedding, label_block, contract_rows, preferred_element_type=jnp.float32
            )
            - log_part[None, :]
        )

    start_state = (
        jnp.full((doc_rows,), -jnp.inf, jnp.float32),
        jnp.zeros((doc_rows,), jnp.float32),
    )
    stored_blocks = jnp.zeros((wide_count, lab_rows, model_width), jnp.bfloat16)

    def visit_block(source, label_block, carry):
        stored, row_state = carry
        stored = lax.dynamic_update_index_in_dim(stored, label_block, source, 0)
        return (stored, absorb(row_state, block_logits(label_block, log_expect[source])))

    def travel(cycle_step, carry):
        label_block, stored, row_state = carry
        source = (wide_place - cycle_step) % wide_count
        stored, row_state = visit_block(source, label_block, (stored, row_state))
        label_block = from_behind(label_block, "wide", 1)
        return (label_block, stored, row_state)

    label_block, stored_blocks, row_state = lax.fori_loop(
        0, wide_count - 1, travel, (label_weight, stored_blocks, start_state)
    )
    stored_blocks, row_state = visit_block(
        (wide_place + 1) % wide_count, label_block, (stored_blocks, row_state)
    )
    run_max, run_sum = row_state
    row_top = lax.pmax(run_max, "narrow")
    row_total = lax.psum(run_sum * jnp.exp(run_max - row_top), "narrow")
    log_total = row_top + jnp.log(row_total)
    per_doc = positive_cols.shape[1]

    def gradient_block(source):
        label_block = stored_blocks[source]
        logits = block_logits(label_block, log_expect[source])
        columns = (source * narrow_count + narrow_place) * lab_rows + offsets
        positive_hits = jnp.sum(
            (positive_cols[:, :, None] == columns[None, None, :]).astype(jnp.float32), axis=1
        )
        grad_logits = (jnp.exp(logits - log_total[:, None]) - positive_hits / per_doc).astype(
            jnp.bfloat16
        )
        return (label_block, grad_logits)

    zero_docs = jnp.zeros((doc_rows, model_width), jnp.float32)

    def carry_home(cycle_step, carry):
        home_sum, embed_back = carry
        source = (wide_place - cycle_step - 1) % wide_count
        label_block, grad_logits = gradient_block(source)
        home_sum = home_sum + lax.dot_general(
            grad_logits, embedding, contract_first, preferred_element_type=jnp.float32
        )
        embed_back = embed_back + jnp.dot(
            grad_logits, label_block, preferred_element_type=jnp.float32
        )
        home_sum = from_behind(home_sum, "wide", 1)
        return (home_sum, embed_back)

    home_sum, embed_back = lax.fori_loop(
        0, wide_count - 1, carry_home, (jnp.zeros((lab_rows, model_width), jnp.float32), zero_docs)
    )
    label_block, grad_logits = gradient_block(wide_place)
    label_grad = home_sum + lax.dot_general(
        grad_logits, embedding, contract_first, preferred_element_type=jnp.float32
    )
    embed_back = embed_back + jnp.dot(grad_logits, label_block, preferred_element_type=jnp.float32)
    embed_grad = lax.psum(embed_back, "narrow").astype(jnp.bfloat16)
    act_grad = lax.dot_general(
        embed_grad, down_weight, contract_rows, preferred_element_type=jnp.float32
    )
    _, gelu_pull = jax.vjp(partial(jax.nn.gelu, approximate=False), pre_act)
    pre_grad = gelu_pull(act_grad)[0].astype(jnp.bfloat16)
    down_term = lax.dot_general(
        hidden, embed_grad, contract_first, preferred_element_type=jnp.float32
    )
    down_grad = lax.psum_scatter(down_term, "wide", scatter_dimension=1, tiled=True)
    up_grad = lax.psum_scatter(
        lax.dot_general(
            documents, pre_grad, contract_first, preferred_element_type=jnp.float32
        ).astype(jnp.bfloat16),
        "wide",
        scatter_dimension=0,
        tiled=True,
    ).astype(jnp.float32)
    return (label_grad, up_grad, down_grad)


def solution(mesh):
    in_specs = (
        P("wide", None),
        P(("wide", "narrow"), None),
        P(("wide", "narrow")),
        P("wide", None),
        P(None, "narrow"),
        P("narrow", None),
    )
    out_specs = (P(("wide", "narrow"), None), P("wide", "narrow"), P("narrow", "wide"))
    return jax.shard_map(local, mesh=mesh, in_specs=in_specs, out_specs=out_specs, check_vma=False)
```

profile of v0, /device:TPU:2, one launch (start us, length us, event | category | flops | bytes accessed | tf_op | source)
XLA Modules:
  0.0 886.5 jit_solution(16799616201651053948)
XLA Ops:
  7.2 4.4 multiply_convert_fusion
  11.6 2.3 fusion.54
  14.6 21.3 %all-gather = s32[16,1,128]{2,1,0:T(1,128)S(1)} all-gather(s32[1,1,128]{2,1,0:T(1,128)S(1)} %bitcast.87), channel_id=1, replica_groups=mesh['wide'=16,'narrow'=16] {'wide'}, dimensions={0}, use_global_device_ids=true | all-gather | bytes 8704 | tf_op jit(solution)/shard_map/all_gather | solution.py:49
  36.8 143.4 %all-reduce.3.cloned.1.call-done = f32[1024,768]{1,0:T(8,128)} async-done(((f32[1024,768]{1,0:T(8,128)}), f32[1024,768]{1,0:T(8,128)}) %all-reduce.3.cloned.1.call-update) | async-done | bytes 3145744 | tf_op jit(solution)/shard_map/psum | solution.py:47
  180.2 2.7 add_convert_fusion
  182.9 2.0 broadcast_in_dim.47
  184.9 119.8 %while.40 = (s32[]{:T(128)}, bf16[128,768]{1,0:T(8,128)(2,1)S(1)}, bf16[16,128,768]{2,1,0:T(8,128)(2,1)}, f32[1024]{0:T(1024)S(1)}, f32[1024]{0:T(1024)S(1)}, /*...) while((s32[]{:T(128)}, bf16[128,768]{1,0:T(8,128)(2,1)S(1)}, ...), condition=%wide.region_4.5_spmd.clone, body=%wide.region_1.4_spmd.clone.sunk | while | flops 201856016 | bytes 4446027 | solution.py:79
  186.6 3.6 collective-permute-done
  191.8 3.5 collective-permute-done
  197.0 3.5 collective-permute-done
  202.2 5.7 collective-permute-done
  209.5 7.1 collective-permute-done
  218.3 7.2 collective-permute-done
  227.1 7.1 collective-permute-done
  235.9 7.2 collective-permute-done
  244.7 7.2 collective-permute-done
  253.6 7.1 collective-permute-done
  262.3 7.2 collective-permute-done
  271.2 7.2 collective-permute-done
  280.0 7.2 collective-permute-done
  288.8 7.2 collective-permute-done
  297.6 7.2 collective-permute-done
  306.1 32.9 %pmax.7 = f32[1024]{0:T(1024)S(1)} all-reduce(f32[1024]{0:T(1024)S(1)} %max.15), channel_id=1, replica_groups=mesh['wide'=16,'narrow'=16] {'narrow'}, use_global_device_ids=true, to_apply=%region_6.7 | all-reduce | flops 1024 | bytes 8192 | tf_op jit(solution)/shard_map/pmax | solution.py:86
  339.1 30.6 %psum.22 = f32[1024]{0:T(1024)S(1)} all-reduce(f32[1024]{0:T(1024)S(1)} %exponential_multiply_fusion), channel_id=1, replica_groups=mesh['wide'=16,'narrow'=16] {'narrow'}, use_global_device_ids=true, to_apply=%region_8.9 | all-reduce | flops 1024 | bytes 8192 | tf_op jit(solution)/shard_map/psum | solution.py:87
  369.7 2.2 fusion.17
  372.0 208.7 %while.41 = (s32[]{:T(128)}, f32[128,768]{1,0:T(8,128)S(1)}, f32[1024,768]{1,0:T(8,128)}, s32[]{:T(128)}, bf16[16,128,768]{2,1,0:T(8,128)(2,1)}, /*index=5*/bf16...) while((s32[]{:T(128)}, f32[128,768]{1,0:T(8,128)S(1)}, ...), condition=%wide.region_11.12_spmd.clone, body=%wide.region_9.11_spmd.clone.sunk | while | flops 607748224 | bytes 15096738 | solution.py:118
  373.2 1.6 fusion.98
  375.3 3.2 select_add_fusion.2
  378.5 4.0 collective-permute-done.1
  383.6 1.6 fusion.98
  385.7 4.3 select_add_fusion.2
  390.0 8.4 collective-permute-done.1
  401.6 4.3 select_add_fusion.2
  405.9 6.5 collective-permute-done.1
  415.6 4.3 select_add_fusion.2
  419.9 6.5 collective-permute-done.1
  429.6 4.3 select_add_fusion.2
  433.9 6.5 collective-permute-done.1
  443.7 4.3 select_add_fusion.2
  447.9 6.5 collective-permute-done.1
  457.7 4.3 select_add_fusion.2
  462.0 6.5 collective-permute-done.1
  471.7 4.3 select_add_fusion.2
  476.0 6.5 collective-permute-done.1
  485.7 4.3 select_add_fusion.2
  490.0 6.5 collective-permute-done.1
  499.7 4.3 select_add_fusion.2
  504.0 6.5 collective-permute-done.1
  513.8 4.3 select_add_fusion.2
  518.0 6.5 collective-permute-done.1
  527.8 4.3 select_add_fusion.2
  532.1 6.5 collective-permute-done.1
  541.8 4.3 select_add_fusion.2
  546.1 6.5 collective-permute-done.1
  555.8 4.3 select_add_fusion.2
  560.1 6.5 collective-permute-done.1
  569.8 4.3 select_add_fusion.2
  574.1 6.5 collective-permute-done.1
  580.6 4.3 convolution_add_fusion.1
  585.0 129.1 %all-reduce.4 = bf16[1024,768]{1,0:T(8,128)(2,1)} all-reduce(f32[1024,768]{1,0:T(8,128)} %convolution_add_fusion.1), channel_id=1, replica_groups=mesh['wide'=16,'narrow'=16] {'narrow'}, use_global_device_ids=true, to_apply=%region_13.14 | all-reduce | flops 786432 | bytes 4718592 | tf_op jit(solution)/shard_map/psum | solution.py:126
  714.1 4.7 fusion.18
  719.8 3.0 fusion.55
  724.0 78.4 %reduce-scatter.7.cloned.1.call-done = bf16[48,192]{1,0:T(8,128)(2,1)} async-done(((bf16[768,192]{1,0:T(8,128)(2,1)}), bf16[48,192]{1,0:T(8,128)(2,1)}) %reduce-scatter.7.cloned.1.call-update) | async-done | bytes 18448
  804.0 76.0 %reduce-scatter.5.cloned.1.call-done = f32[192,48]{0,1:T(8,128)} async-done(((f32[192,768]{0,1:T(8,128)}), f32[192,48]{0,1:T(8,128)}) %reduce-scatter.5.cloned.1.call-update) | async-done | bytes 36880 | tf_op jit(solution)/shard_map/reduce_scatter | solution.py:135
  (276 shorter events, 74.6 us)
Async XLA Ops:
  7.2 4.5 copy-start
  7.2 173.0 %all-reduce.3.cloned.1.call-start = ((), (), s32[]{:S(2)}) async-start(), calls=%async_computation.2 | async-start | bytes 6291456 | tf_op jit(solution)/shard_map/psum | solution.py:47
  11.6 2.4 copy-start.3
  14.0 0.7 copy-start.6
  14.0 22.0 %copy-start.5 = (s32[1024,4]{0,1:T(4,128)S(1)}, s32[1024,4]{0,1:T(4,128)}, u32[]{:S(2)}) copy-start(s32[1024,4]{0,1:T(4,128)} %param.13) | copy-start | bytes 49156
  14.0 788.4 %reduce-scatter.7.cloned.1.call-start = ((), (), s32[]{:S(2)}) async-start(), calls=%async_computation.4 | async-start | bytes 417792
  182.9 2.0 copy-start.1
  184.9 5.2 collective-permute-start
  190.1 5.2 collective-permute-start
  195.3 5.2 collective-permute-start
  200.5 7.4 collective-permute-start
  207.9 8.8 collective-permute-start
  216.7 8.8 collective-permute-start
  225.5 8.8 collective-permute-start
  234.3 8.8 collective-permute-start
  243.1 8.8 collective-permute-start
  251.9 8.8 collective-permute-start
  260.7 8.8 collective-permute-start
  269.5 8.8 collective-permute-start
  278.3 8.8 collective-permute-start
  287.1 8.8 collective-permute-start
  295.9 8.8 collective-permute-start
  375.2 7.3 collective-permute-start.1
  385.6 12.8 %collective-permute-start.1 = (f32[128,768]{1,0:T(8,128)S(1)}, f32[128,768]{1,0:T(8,128)S(1)}, u32[]{:S(2)}, u32[]{:S(2)}) collective-permute-start(f32[128,768]{1,0:T(8,128)S(1)} %convolution_add_fusion.4), channel_id=1, source_target_pairs={{240,0},{0,16},{16,32},{32,48},{48,64},{64,80},{80,96},{96,112},{1... | collective-permute-start | bytes 1179656 | tf_op jit(solution)/shard_map/while/body/eval_jaxpr/ppermute | solution.py:13
  401.5 10.9 %collective-permute-start.1 = (f32[128,768]{1,0:T(8,128)S(1)}, f32[128,768]{1,0:T(8,128)S(1)}, u32[]{:S(2)}, u32[]{:S(2)}) collective-permute-start(f32[128,768]{1,0:T(8,128)S(1)} %convolution_add_fusion.4), channel_id=1, source_target_pairs={{240,0},{0,16},{16,32},{32,48},{48,64},{64,80},{80,96},{96,112},{1... | collective-permute-start | bytes 1179656 | tf_op jit(solution)/shard_map/while/body/eval_jaxpr/ppermute | solution.py:13
  415.5 10.9 %collective-permute-start.1 = (f32[128,768]{1,0:T(8,128)S(1)}, f32[128,768]{1,0:T(8,128)S(1)}, u32[]{:S(2)}, u32[]{:S(2)}) collective-permute-start(f32[128,768]{1,0:T(8,128)S(1)} %convolution_add_fusion.4), channel_id=1, source_target_pairs={{240,0},{0,16},{16,32},{32,48},{48,64},{64,80},{80,96},{96,112},{1... | collective-permute-start | bytes 1179656 | tf_op jit(solution)/shard_map/while/body/eval_jaxpr/ppermute | solution.py:13
  429.5 10.9 %collective-permute-start.1 = (f32[128,768]{1,0:T(8,128)S(1)}, f32[128,768]{1,0:T(8,128)S(1)}, u32[]{:S(2)}, u32[]{:S(2)}) collective-permute-start(f32[128,768]{1,0:T(8,128)S(1)} %convolution_add_fusion.4), channel_id=1, source_target_pairs={{240,0},{0,16},{16,32},{32,48},{48,64},{64,80},{80,96},{96,112},{1... | collective-permute-start | bytes 1179656 | tf_op jit(solution)/shard_map/while/body/eval_jaxpr/ppermute | solution.py:13
  443.6 10.9 %collective-permute-start.1 = (f32[128,768]{1,0:T(8,128)S(1)}, f32[128,768]{1,0:T(8,128)S(1)}, u32[]{:S(2)}, u32[]{:S(2)}) collective-permute-start(f32[128,768]{1,0:T(8,128)S(1)} %convolution_add_fusion.4), channel_id=1, source_target_pairs={{240,0},{0,16},{16,32},{32,48},{48,64},{64,80},{80,96},{96,112},{1... | collective-permute-start | bytes 1179656 | tf_op jit(solution)/shard_map/while/body/eval_jaxpr/ppermute | solution.py:13
  457.6 10.9 %collective-permute-start.1 = (f32[128,768]{1,0:T(8,128)S(1)}, f32[128,768]{1,0:T(8,128)S(1)}, u32[]{:S(2)}, u32[]{:S(2)}) collective-permute-start(f32[128,768]{1,0:T(8,128)S(1)} %convolution_add_fusion.4), channel_id=1, source_target_pairs={{240,0},{0,16},{16,32},{32,48},{48,64},{64,80},{80,96},{96,112},{1... | collective-permute-start | bytes 1179656 | tf_op jit(solution)/shard_map/while/body/eval_jaxpr/ppermute | solution.py:13
  471.6 10.9 %collective-permute-start.1 = (f32[128,768]{1,0:T(8,128)S(1)}, f32[128,768]{1,0:T(8,128)S(1)}, u32[]{:S(2)}, u32[]{:S(2)}) collective-permute-start(f32[128,768]{1,0:T(8,128)S(1)} %convolution_add_fusion.4), channel_id=1, source_target_pairs={{240,0},{0,16},{16,32},{32,48},{48,64},{64,80},{80,96},{96,112},{1... | collective-permute-start | bytes 1179656 | tf_op jit(solution)/shard_map/while/body/eval_jaxpr/ppermute | solution.py:13
  485.6 10.9 %collective-permute-start.1 = (f32[128,768]{1,0:T(8,128)S(1)}, f32[128,768]{1,0:T(8,128)S(1)}, u32[]{:S(2)}, u32[]{:S(2)}) collective-permute-start(f32[128,768]{1,0:T(8,128)S(1)} %convolution_add_fusion.4), channel_id=1, source_target_pairs={{240,0},{0,16},{16,32},{32,48},{48,64},{64,80},{80,96},{96,112},{1... | collective-permute-start | bytes 1179656 | tf_op jit(solution)/shard_map/while/body/eval_jaxpr/ppermute | solution.py:13
  499.6 10.9 %collective-permute-start.1 = (f32[128,768]{1,0:T(8,128)S(1)}, f32[128,768]{1,0:T(8,128)S(1)}, u32[]{:S(2)}, u32[]{:S(2)}) collective-permute-start(f32[128,768]{1,0:T(8,128)S(1)} %convolution_add_fusion.4), channel_id=1, source_target_pairs={{240,0},{0,16},{16,32},{32,48},{48,64},{64,80},{80,96},{96,112},{1... | collective-permute-start | bytes 1179656 | tf_op jit(solution)/shard_map/while/body/eval_jaxpr/ppermute | solution.py:13
  513.7 10.9 %collective-permute-start.1 = (f32[128,768]{1,0:T(8,128)S(1)}, f32[128,768]{1,0:T(8,128)S(1)}, u32[]{:S(2)}, u32[]{:S(2)}) collective-permute-start(f32[128,768]{1,0:T(8,128)S(1)} %convolution_add_fusion.4), channel_id=1, source_target_pairs={{240,0},{0,16},{16,32},{32,48},{48,64},{64,80},{80,96},{96,112},{1... | collective-permute-start | bytes 1179656 | tf_op jit(solution)/shard_map/while/body/eval_jaxpr/ppermute | solution.py:13
  527.7 10.9 %collective-permute-start.1 = (f32[128,768]{1,0:T(8,128)S(1)}, f32[128,768]{1,0:T(8,128)S(1)}, u32[]{:S(2)}, u32[]{:S(2)}) collective-permute-start(f32[128,768]{1,0:T(8,128)S(1)} %convolution_add_fusion.4), channel_id=1, source_target_pairs={{240,0},{0,16},{16,32},{32,48},{48,64},{64,80},{80,96},{96,112},{1... | collective-permute-start | bytes 1179656 | tf_op jit(solution)/shard_map/while/body/eval_jaxpr/ppermute | solution.py:13
  541.7 10.9 %collective-permute-start.1 = (f32[128,768]{1,0:T(8,128)S(1)}, f32[128,768]{1,0:T(8,128)S(1)}, u32[]{:S(2)}, u32[]{:S(2)}) collective-permute-start(f32[128,768]{1,0:T(8,128)S(1)} %convolution_add_fusion.4), channel_id=1, source_target_pairs={{240,0},{0,16},{16,32},{32,48},{48,64},{64,80},{80,96},{96,112},{1... | collective-permute-start | bytes 1179656 | tf_op jit(solution)/shard_map/while/body/eval_jaxpr/ppermute | solution.py:13
  555.7 10.9 %collective-permute-start.1 = (f32[128,768]{1,0:T(8,128)S(1)}, f32[128,768]{1,0:T(8,128)S(1)}, u32[]{:S(2)}, u32[]{:S(2)}) collective-permute-start(f32[128,768]{1,0:T(8,128)S(1)} %convolution_add_fusion.4), channel_id=1, source_target_pairs={{240,0},{0,16},{16,32},{32,48},{48,64},{64,80},{80,96},{96,112},{1... | collective-permute-start | bytes 1179656 | tf_op jit(solution)/shard_map/while/body/eval_jaxpr/ppermute | solution.py:13
  569.7 10.9 %collective-permute-start.1 = (f32[128,768]{1,0:T(8,128)S(1)}, f32[128,768]{1,0:T(8,128)S(1)}, u32[]{:S(2)}, u32[]{:S(2)}) collective-permute-start(f32[128,768]{1,0:T(8,128)S(1)} %convolution_add_fusion.4), channel_id=1, source_target_pairs={{240,0},{0,16},{16,32},{32,48},{48,64},{64,80},{80,96},{96,112},{1... | collective-permute-start | bytes 1179656 | tf_op jit(solution)/shard_map/while/body/eval_jaxpr/ppermute | solution.py:13
  714.1 5.7 copy-start.4
  719.7 3.1 copy-start.2
  719.7 160.3 %reduce-scatter.5.cloned.1.call-start = ((), (), s32[]{:S(2)}) async-start(), calls=%async_computation.3 | async-start | bytes 835584 | tf_op jit(solution)/shard_map/reduce_scatter | solution.py:135
Sparse Core Ops, SparseCore 0:
  14.1 166.0 all-reduce.2
  719.8 82.5 reduce-scatter.6
  807.0 72.8 reduce-scatter.4
where the time goes:
time: 888 us; the launch traced here: 886 us
  waiting for transfers between devices  490 us (55%)
  blocking collectives  214 us (24%)
  matrix products  126 us (14%)
  local copies, waits for them, and re-layouts  19.7 us (2%)
  other arithmetic  18.7 us (2%)
  between operations  13.9 us (2%)
    ppermute x30, waiting for transfers between devices, from_behind(): return lax.ppermute(block, axis, route)  192 us
    psum x1, waiting for transfers between devices, local(): summed = lax.psum(partial_out, 'narrow')  143 us
    psum x1, blocking collectives, local(): embed_grad = lax.psum(embed_back, 'narrow').astype(jnp.bfloat16)  129 us
    unnamed x4, waiting for transfers between devices  78.5 us
    reduce_scatter x1, waiting for transfers between devices, local(): lax.psum_scatter(down_term, 'wide', scatter_dimension=1, tiled=True)  76 us
    dot_general x15, matrix products, carry_home(): jnp.dot(grad_logits, label_block, preferred_element_type=jnp.float32)  63.1 us
    dot_general x32, matrix products, block_logits(): lax.dot_general(embedding, label_block, contract_rows, preferred_element_...  36.8 us
    pmax x1, blocking collectives, local(): row_top = lax.pmax(run_max, 'narrow')  32.9 us
  transfers between devices with their start and end apart: 33, of which 33 were waited for; matrix products, arithmetic and copies ran while one was open for 10% of the time, Pallas kernels for 0%

commit v1 on v0

--- a/solution.py
+++ b/solution.py
@@ -44,7 +44,7 @@
     pre_act = jnp.dot(documents, up_weight, preferred_element_type=jnp.float32)
     hidden = jax.nn.gelu(pre_act, approximate=False).astype(jnp.bfloat16)
     partial_out = jnp.dot(hidden, down_weight, preferred_element_type=jnp.float32)
-    summed = lax.psum(partial_out, "narrow")
+    summed = jnp.sum(lax.all_gather(partial_out, "narrow"), axis=0)
     embedding = (documents.astype(jnp.float32) + summed).astype(jnp.bfloat16)
     all_ranks = lax.all_gather(sample_ids, "wide", axis=0, tiled=True)
     log_expect = expected_log(all_ranks, sampled).reshape(wide_count, lab_rows)

time: 888 us -> 1770 us (1.99)
  waiting for transfers between devices: 490 us -> 1350 us
  other arithmetic: 18.7 us -> 38.2 us
    all_gather x0 -> x1, waiting for transfers between devices: none -> 1010 us  [local(): summed = jnp.sum(lax.all_gather(partial_out, 'narrow'), axis=0)]
    psum x1 -> x0, waiting for transfers between devices: 143 us -> none  [local(): summed = lax.psum(partial_out, 'narrow')]
    reduce_sum x0 -> x1, other arithmetic: none -> 19.5 us  [local(): summed = jnp.sum(lax.all_gather(partial_out, 'narrow'), axis=0)]
  transfers between devices with their start and end apart: 33 -> 33, of which waited for: 33 -> 33; matrix products, arithmetic and copies ran while one was open for 10% -> 5% of each run, Pallas kernels for 0% -> 0%
where the time goes in v1:
time: 1770 us
  waiting for transfers between devices  1350 us (76%)
  blocking collectives  214 us (12%)
  matrix products  125 us (7%)
  other arithmetic  38.2 us (2%)
  local copies, waits for them, and re-layouts  20.4 us (1%)
    all_gather x1, waiting for transfers between devices, local(): summed = jnp.sum(lax.all_gather(partial_out, 'narrow'), axis=0)  1010 us
    ppermute x30, waiting for transfers between devices, from_behind(): return lax.ppermute(block, axis, route)  193 us
    psum x1, blocking collectives, local(): embed_grad = lax.psum(embed_back, 'narrow').astype(jnp.bfloat16)  129 us
    unnamed x4, waiting for transfers between devices  78.9 us
    reduce_scatter x1, waiting for transfers between devices, local(): lax.psum_scatter(down_term, 'wide', scatter_dimension=1, tiled=True)  76 us
    dot_general x15, matrix products, carry_home(): jnp.dot(grad_logits, label_block, preferred_element_type=jnp.float32)  62.4 us
    dot_general x32, matrix products, block_logits(): lax.dot_general(embedding, label_block, contract_rows, preferred_element_...  36.8 us
  transfers between devices with their start and end apart: 33, of which 33 were waited for; matrix products, arithmetic and copies ran while one was open for 5% of the time, Pallas kernels for 0%

profile of v1, /device:TPU:2, one launch (start us, length us, event | category | flops | bytes accessed | tf_op | source)
XLA Modules:
  0.0 1769.2 jit_solution(12904130135525270723)
XLA Ops:
  7.2 4.4 multiply_convert_fusion
  12.4 2.3 fusion.54
  15.3 21.3 %all-gather.1 = s32[16,1,128]{2,1,0:T(1,128)S(1)} all-gather(s32[1,1,128]{2,1,0:T(1,128)S(1)} %bitcast.89), channel_id=1, replica_groups=mesh['wide'=16,'narrow'=16] {'wide'}, dimensions={0}, use_global_device_ids=true | all-gather | bytes 8704 | tf_op jit(solution)/shard_map/all_gather | solution.py:49
  37.5 1005.3 %all-gather.4.cloned.1.call-done = f32[16384,768]{1,0:T(8,128)} async-done(((f32[1024,768]{1,0:T(8,128)}), f32[16384,768]{1,0:T(8,128)}) %all-gather.4.cloned.1.call-update) | async-done | bytes 50331664 | tf_op jit(solution)/shard_map/all_gather | solution.py:47
  1042.9 19.5 %reduce_sum.59 = f32[1024,768]{1,0:T(8,128)} reduce(f32[16,1024,768]{2,1,0:T(8,128)} %bitcast.87, f32[]{:T(128)} %constant.204.clone.1), dimensions={0}, to_apply=%region_0.0 | reduce | flops 11796480 | bytes 53477380 | tf_op jit(solution)/shard_map/reduce_sum | solution.py:47
  1062.4 2.7 add_convert_fusion
  1065.1 2.0 broadcast_in_dim.47
  1067.0 119.6 %while.40 = (s32[]{:T(128)}, bf16[128,768]{1,0:T(8,128)(2,1)S(1)}, bf16[16,128,768]{2,1,0:T(8,128)(2,1)}, f32[1024]{0:T(1024)S(1)}, f32[1024]{0:T(1024)S(1)}, /*...) while((s32[]{:T(128)}, bf16[128,768]{1,0:T(8,128)(2,1)S(1)}, ...), condition=%wide.region_4.5_spmd.clone, body=%wide.region_1.4_spmd.clone.sunk | while | flops 201856016 | bytes 4446027 | solution.py:79
  1068.7 3.6 collective-permute-done
  1073.9 3.5 collective-permute-done
  1079.1 3.5 collective-permute-done
  1084.3 5.6 collective-permute-done
  1091.5 7.2 collective-permute-done
  1100.3 7.2 collective-permute-done
  1109.1 7.2 collective-permute-done
  1117.9 7.1 collective-permute-done
  1126.7 7.2 collective-permute-done
  1135.5 7.2 collective-permute-done
  1144.3 7.2 collective-permute-done
  1153.1 7.1 collective-permute-done
  1161.9 7.2 collective-permute-done
  1170.7 7.2 collective-permute-done
  1179.5 7.2 collective-permute-done
  1187.3 33.1 %pmax.7 = f32[1024]{0:T(1024)S(1)} all-reduce(f32[1024]{0:T(1024)S(1)} %max.15), channel_id=1, replica_groups=mesh['wide'=16,'narrow'=16] {'narrow'}, use_global_device_ids=true, to_apply=%region_6.7 | all-reduce | flops 1024 | bytes 8192 | tf_op jit(solution)/shard_map/pmax | solution.py:86
  1220.6 30.8 %psum.14 = f32[1024]{0:T(1024)S(1)} all-reduce(f32[1024]{0:T(1024)S(1)} %exponential_multiply_fusion), channel_id=1, replica_groups=mesh['wide'=16,'narrow'=16] {'narrow'}, use_global_device_ids=true, to_apply=%region_8.9 | all-reduce | flops 1024 | bytes 8192 | tf_op jit(solution)/shard_map/psum | solution.py:87
  1252.1 2.2 fusion.17
  1254.3 208.6 %while.41 = (s32[]{:T(128)}, f32[128,768]{1,0:T(8,128)S(1)}, f32[1024,768]{1,0:T(8,128)}, s32[]{:T(128)}, bf16[16,128,768]{2,1,0:T(8,128)(2,1)}, /*index=5*/bf16...) while((s32[]{:T(128)}, f32[128,768]{1,0:T(8,128)S(1)}, ...), condition=%wide.region_11.12_spmd.clone, body=%wide.region_9.11_spmd.clone.sunk | while | flops 607748224 | bytes 15096738 | solution.py:118
  1257.6 3.2 select_add_fusion.2
  1260.7 4.0 collective-permute-done.1
  1265.9 1.6 fusion.98
  1268.0 4.2 select_add_fusion.2
  1272.2 8.4 collective-permute-done.1
  1283.8 4.2 select_add_fusion.2
  1288.1 6.6 collective-permute-done.1
  1297.9 4.2 select_add_fusion.2
  1302.1 6.6 collective-permute-done.1
  1311.9 4.2 select_add_fusion.2
  1316.1 6.6 collective-permute-done.1
  1325.9 4.2 select_add_fusion.2
  1330.1 6.6 collective-permute-done.1
  1339.9 4.2 select_add_fusion.2
  1344.1 6.6 collective-permute-done.1
  1353.9 4.2 select_add_fusion.2
  1358.2 6.6 collective-permute-done.1
  1368.0 4.2 select_add_fusion.2
  1372.2 6.6 collective-permute-done.1
  1382.0 4.2 select_add_fusion.2
  1386.2 6.6 collective-permute-done.1
  1396.0 4.2 select_add_fusion.2
  1400.2 6.6 collective-permute-done.1
  1410.0 4.2 select_add_fusion.2
  1414.3 6.6 collective-permute-done.1
  1424.0 4.2 select_add_fusion.2
  1428.3 6.6 collective-permute-done.1
  1438.1 4.2 select_add_fusion.2
  1442.3 6.6 collective-permute-done.1
  1452.1 4.2 select_add_fusion.2
  1456.3 6.6 collective-permute-done.1
  1462.9 4.3 convolution_add_fusion.1
  1467.2 129.0 %all-reduce.1 = bf16[1024,768]{1,0:T(8,128)(2,1)} all-reduce(f32[1024,768]{1,0:T(8,128)} %convolution_add_fusion.1), channel_id=1, replica_groups=mesh['wide'=16,'narrow'=16] {'narrow'}, use_global_device_ids=true, to_apply=%region_13.14 | all-reduce | flops 786432 | bytes 4718592 | tf_op jit(solution)/shard_map/psum | solution.py:126
  1596.2 4.7 fusion.18
  1601.9 3.0 fusion.55
  1606.2 78.9 %reduce-scatter.7.cloned.1.call-done = bf16[48,192]{1,0:T(8,128)(2,1)} async-done(((bf16[768,192]{1,0:T(8,128)(2,1)}), bf16[48,192]{1,0:T(8,128)(2,1)}) %reduce-scatter.7.cloned.1.call-update) | async-done | bytes 18448
  1686.6 76.0 %reduce-scatter.5.cloned.1.call-done = f32[192,48]{0,1:T(8,128)} async-done(((f32[192,768]{0,1:T(8,128)}), f32[192,48]{0,1:T(8,128)}) %reduce-scatter.5.cloned.1.call-update) | async-done | bytes 36880 | tf_op jit(solution)/shard_map/reduce_scatter | solution.py:135
  (277 shorter events, 76.9 us)
Async XLA Ops:
  7.2 5.3 copy-start
  7.2 1035.7 %all-gather.4.cloned.1.call-start = ((), (), s32[]{:S(2)}) async-start(), calls=%async_computation.3 | async-start | bytes 53477376 | tf_op jit(solution)/shard_map/all_gather | solution.py:47
  11.7 0.7 copy-start.3
  14.7 0.7 copy-start.6
  14.7 22.0 %copy-start.5 = (s32[1024,4]{0,1:T(4,128)S(1)}, s32[1024,4]{0,1:T(4,128)}, u32[]{:S(2)}) copy-start(s32[1024,4]{0,1:T(4,128)} %param.13) | copy-start | bytes 49156
  14.7 1670.3 %reduce-scatter.7.cloned.1.call-start = ((), (), s32[]{:S(2)}) async-start(), calls=%async_computation.4 | async-start | bytes 417792
  1065.1 2.0 copy-start.1
  1067.1 5.2 collective-permute-start
  1072.3 5.2 collective-permute-start
  1077.4 5.2 collective-permute-start
  1082.6 7.2 collective-permute-start
  1089.8 8.8 collective-permute-start
  1098.6 8.8 collective-permute-start
  1107.5 8.8 collective-permute-start
  1116.3 8.8 collective-permute-start
  1125.1 8.8 collective-permute-start
  1133.9 8.8 collective-permute-start
  1142.7 8.8 collective-permute-start
  1151.5 8.8 collective-permute-start
  1160.3 8.8 collective-permute-start
  1169.1 8.8 collective-permute-start
  1177.9 8.8 collective-permute-start
  1257.5 7.3 collective-permute-start.1
  1267.9 12.7 collective-permute-start.1
  1283.7 10.9 collective-permute-start.1
  1297.8 10.9 collective-permute-start.1
  1311.8 10.9 collective-permute-start.1
  1325.8 10.9 collective-permute-start.1
  1339.8 10.9 collective-permute-start.1
  1353.8 10.9 collective-permute-start.1
  1367.9 10.9 collective-permute-start.1
  1381.9 10.9 collective-permute-start.1
  1395.9 10.9 collective-permute-start.1
  1409.9 10.9 collective-permute-start.1
  1423.9 10.9 collective-permute-start.1
  1438.0 10.9 collective-permute-start.1
  1452.0 10.9 collective-permute-start.1
  1596.2 5.7 copy-start.4
  1601.9 3.1 copy-start.2
  1601.9 160.8 %reduce-scatter.5.cloned.1.call-start = ((), (), s32[]{:S(2)}) async-start(), calls=%async_computation.2 | async-start | bytes 835584 | tf_op jit(solution)/shard_map/reduce_scatter | solution.py:135
Sparse Core Ops, SparseCore 0:
  14.8 1028.0 all-gather.3
  1602.0 82.9 reduce-scatter.6
  1689.7 72.9 reduce-scatter.4
